TPU v7x, 256 devices: a whole 4x4x8 slice. The times are simulated.
256 devices in a mesh: rep: 16 (over y_hi, z), fsdp: 16 (over x, y_lo, core).
Axes of the slice: x: 4, y: 4 (y_hi: 2, y_lo: 2; y = y_hi * 2 + y_lo), z: 8, core: 2. Of those that a mesh axis runs over, the one named last changes fastest.
Arguments:
- tokens: bfloat16 [131072, 4096], P(('rep', 'fsdp')), may hold values from -6 to 6
- gate_pre: bfloat16 [131072, 768], P(('rep', 'fsdp')), may hold values from -8 to 8
- upstream: bfloat16 [131072, 768], P(('rep', 'fsdp')), may hold values from -6 to 6
- slow: float32 [16, 4096, 768], P('rep', 'fsdp'), may hold values from -6 to 6
- inner_mom: bfloat16 [16, 4096, 768], P('rep', 'fsdp'), may hold values from -6 to 6
- outer_mom: bfloat16 [16, 4096, 768], P('rep', 'fsdp'), may hold values from -3 to 3
- pairing: int32 [16], replicated, may hold values from 0 to 15, as said below
Outputs:
- gate_grad: bfloat16 [131072, 768], P(('rep', 'fsdp'))
- inner_new: bfloat16 [16, 4096, 768], P('rep', 'fsdp')
- outer_new: bfloat16 [16, 4096, 768], P('rep', 'fsdp')
- slow_new: float32 [16, 4096, 768], P('rep', 'fsdp')
Inputs may be any that keep to these rules, and one draw needn't show every extreme that they name: pairing[i] = i XOR p for one p of 1 to 15 shared by all i, so pairing[pairing[i]] = i.
All inputs are finite; a program needn't handle non-finite values.
Results may differ from a plain program's by a relative error of at most 0.009.
Values may be sent and summed in bfloat16 or wider, within the bound.
No kernel may reach another device: no remote copies, remote signals or barrier semaphores. Data moves between devices by JAX's collectives and lax.ppermute only.
A program may use at most 128 MiB of HBM per device.

v0:
```python
import jax
import jax.numpy as jnp
from jax import lax
from jax.experimental import pallas as pl
from jax.experimental.pallas import tpu as pltpu
from jax.sharding import Mesh, PartitionSpec as P


D = 4096
COLS = 768
HALF = COLS // 2
BLOCK = 256
ROWS = 512

inner_beta = 0.9
inner_rate = 0.5
outer_mu = 0.9
outer_rate = 0.7

F32 = jnp.float32
BF16 = jnp.bfloat16
SHAPE = jax.ShapeDtypeStruct
WHOLE = pl.BlockSpec(memory_space=pltpu.VMEM)


def swap(block, axis):
    return lax.ppermute(block, axis, [(0, 1), (1, 0)])


def swap_x(block, distance):
    return lax.ppermute(block, "x", [(i, i ^ distance) for i in range(4)])


def pair_exchange(block, partner_xor):
    def branch(distance):
        route = [(i, i ^ distance) for i in range(16)]
        return lambda value: lax.ppermute(value, ("yh", "z"), route)

    return lax.switch(partner_xor - 1, [branch(d) for d in range(1, 16)], block)


def pick_kernel(order, tokens, out):
    out[...] = tokens[...]


def pick(tokens, order):
    return pl.pallas_call(
        pick_kernel,
        out_shape=SHAPE((ROWS, 8 * BLOCK), BF16),
        grid_spec=pltpu.PrefetchScalarGridSpec(
            num_scalar_prefetch=1,
            grid=(8,),
            in_specs=[pl.BlockSpec((ROWS, BLOCK), lambda i, order: (0, order[i]))],
            out_specs=pl.BlockSpec((ROWS, BLOCK), lambda i, order: (0, i)),
        ),
        cost_estimate=pl.CostEstimate(flops=0, bytes_accessed=2**22, transcendentals=0),
        name="pick",
    )(order, tokens)


def cast_kernel(slow, whole, first, second):
    fast = slow[...].astype(BF16)
    whole[...] = fast
    first[...] = fast[:, :HALF]
    second[...] = fast[:, HALF:]


def cast(slow):
    return pl.pallas_call(
        cast_kernel,
        out_shape=[SHAPE((BLOCK, COLS), BF16)] + [SHAPE((BLOCK, HALF), BF16)] * 2,
        in_specs=[WHOLE],
        out_specs=[WHOLE] * 3,
        cost_estimate=pl.CostEstimate(flops=0, bytes_accessed=2**20, transcendentals=0),
        name="cast",
    )(slow)


def grad_kernel(order, own_tokens, other_tokens, own_grads, other_grads, a0, a1, a2, a3, keep, send):
    step = pl.program_id(0)
    contract = (((0,), (0,)), ((), ()))
    total = lax.dot_general(
        own_tokens[...], own_grads[...], contract, preferred_element_type=F32
    ) + lax.dot_general(other_tokens[...], other_grads[...], contract, preferred_element_type=F32)
    total = total.astype(BF16)
    for distance, out in enumerate((a0, a1, a2, a3)):

        @pl.when(step // 2 == distance)
        def _():
            out[...] = total[:, :HALF]

    for side, out in enumerate((keep, send)):

        @pl.when(lax.rem(step, 2) == side)
        def _():
            out[...] = total[:, HALF:]


def partial_gradient(order, tokens, other_tokens, own_grads, other_grads):
    def piece(distance):
        return pl.BlockSpec(
            (BLOCK, HALF),
            lambda i, order: (jnp.clip(i - 2 * distance, 0, 1), 0),
        )

    grads = pl.BlockSpec((ROWS, COLS), lambda i, order: (0, 0))
    return pl.pallas_call(
        grad_kernel,
        out_shape=[SHAPE((2 * BLOCK, HALF), BF16)] * 4 + [SHAPE((4 * BLOCK, HALF), BF16)] * 2,
        grid_spec=pltpu.PrefetchScalarGridSpec(
            num_scalar_prefetch=1,
            grid=(8,),
            in_specs=[
                pl.BlockSpec((ROWS, BLOCK), lambda i, order: (0, order[i])),
                pl.BlockSpec((ROWS, BLOCK), lambda i, order: (0, i)),
                grads,
                grads,
            ],
            out_specs=[piece(distance) for distance in range(4)]
            + [
                pl.BlockSpec((BLOCK, HALF), lambda i, order: (i // 2, 0)),
                pl.BlockSpec((BLOCK, HALF), lambda i, order: (jnp.maximum(i - 1, 0) // 2, 0)),
            ],
        ),
        cost_estimate=pl.CostEstimate(
            flops=2 * 1024 * 2048 * 768, bytes_accessed=9 * 2**20, transcendentals=0
        ),
        name="weight_gradient",
    )(order, tokens, other_tokens, own_grads, other_grads)


def up_kernel(tokens, pair, x1, x2, x3, near, far, out):
    rows = 128

    @pl.loop(0, ROWS // rows)
    def _(tile):
        here = pl.ds(pl.multiple_of(tile * rows, rows), rows)

        def times(step, count, weight):
            return jnp.dot(
                tokens[here, step * BLOCK : (step + count) * BLOCK],
                weight,
                preferred_element_type=F32,
            )

        total = jnp.zeros((rows, HALF), F32)
        for distance, weight in enumerate((pair, x1, x2, x3)):
            total += times(2 * distance, 2, weight[...])
        out[here, :HALF] = total
        total = jnp.zeros((rows, HALF), F32)
        for side, weight in enumerate((near, far)):
            for distance in range(4):
                total += times(
                    2 * distance + side, 1, weight[distance * BLOCK : (distance + 1) * BLOCK, :]
                )
        out[here, HALF:] = total


def up_partial(tokens, *weights):
    return pl.pallas_call(
        up_kernel,
        out_shape=SHAPE((ROWS, COLS), F32),
        in_specs=[WHOLE] * 7,
        out_specs=WHOLE,
        cost_estimate=pl.CostEstimate(
            flops=2 * 512 * 2048 * 768, bytes_accessed=6 * 2**20, transcendentals=0
        ),
        name="up",
    )(tokens, *weights)


def local(tokens, gate_pre, upstream, slow, inner_mom, outer_mom, pairing):
    weight_scale = float(D) ** (-0.5)
    core = lax.axis_index("core")
    step = jnp.arange(8, dtype=jnp.int32)
    owner = (lax.axis_index("x") ^ (step // 2)) * 2 + (lax.axis_index("yl") ^ (step % 2))
    own_order = owner * 2 + core
    other_order = owner * 2 + (1 - core)
    slow_shard = slow[0]
    fast_weight, weight_a, weight_b = cast(slow_shard)
    partner_xor = pairing[0]

    other_tokens = swap(pick(tokens, other_order), "core")
    own_tokens = pick(tokens, own_order)

    gate_values = gate_pre.astype(F32)
    sigmoid_gate = jax.nn.sigmoid(gate_values)
    upstream_values = upstream.astype(F32)
    grad_rows = (upstream_values * gate_values * sigmoid_gate).astype(BF16)
    factor = (
        upstream_values * sigmoid_gate * (1.0 + gate_values * (1.0 - sigmoid_gate)) * weight_scale
    )
    grad_rows, factor = lax.optimization_barrier((grad_rows, factor))
    other_grads = swap(grad_rows, "core")

    pair = jnp.concatenate([weight_a, swap(weight_a, "yl")])
    near = jnp.concatenate([weight_b] + [swap_x(weight_b, k) for k in (1, 2, 3)])
    weights = [pair] + [swap_x(pair, k) for k in (1, 2, 3)] + [near, swap(near, "yl")]

    a0, a1, a2, a3, keep, send = partial_gradient(
        own_order, tokens, other_tokens, grad_rows, other_grads
    )
    part_a = a0.astype(F32)
    for k, piece in ((1, a1), (2, a2), (3, a3)):
        part_a = part_a + swap_x(piece, k).astype(F32)
    part_a = part_a[:BLOCK] + swap(part_a[BLOCK:].astype(BF16), "yl").astype(F32)
    part_b = keep.astype(F32) + swap(send, "yl").astype(F32)
    part_b = part_b.reshape(4, BLOCK, HALF)
    total_b = part_b[0]
    for k in (1, 2, 3):
        total_b = total_b + swap_x(part_b[k].astype(BF16), k).astype(F32)
    weight_grad = jnp.concatenate([part_a, total_b], 1) * weight_scale

    inner_new = (inner_beta * inner_mom[0].astype(F32) + weight_grad).astype(BF16)
    outer_grad = slow_shard - (fast_weight.astype(F32) - inner_rate * inner_new.astype(F32))
    slow_partner = pair_exchange(fast_weight, partner_xor).astype(F32)
    grad_partner = pair_exchange(outer_grad.astype(BF16), partner_xor).astype(F32)
    mean_slow = 0.5 * (slow_shard + slow_partner)
    mean_grad = 0.5 * (outer_grad + grad_partner)
    outer_new = (outer_mu * outer_mom[0].astype(F32) + mean_grad).astype(BF16)
    slow_new = mean_slow - outer_rate * (mean_grad + outer_mu * outer_new.astype(F32))

    other_up = swap(up_partial(other_tokens, *weights), "core")
    own_up = up_partial(own_tokens, *weights)
    gate_grad = ((own_up + other_up) * factor).astype(BF16)
    return (gate_grad, inner_new[None], outer_new[None], slow_new[None])


def solution(mesh):
    fine = Mesh(mesh.devices.reshape(2, 8, 4, 2, 2), ("yh", "z", "x", "yl", "core"))
    rep, fsdp = ("yh", "z"), ("x", "yl", "core")
    rows = P(rep + fsdp, None)
    state = P(rep, fsdp, None)


    return jax.shard_map(
        local,
        mesh=fine,
        in_specs=(rows, rows, rows, state, state, state, P()),
        out_specs=(rows, state, state, state),
        check_vma=False,
    )
```

profile of v0, /device:TPU:65, one launch (start us, length us, event | category | flops | bytes accessed | tf_op | source)
XLA Modules:
  0.0 130.9 jit_solution(6246879378868283328)
XLA Ops:
  1.2 6.6 %pick.3 = bf16[512,2048]{1,0:T(8,128)(2,1)} custom-call(s32[8]{0:T(128)} %broadcast_add_fusion.order, bf16[512,4096]{1,0:T(8,128)(2,1)} %own_tokens.1), custom_call_target="tpu_custom_call" | custom-call | bytes 4194304 | tf_op jit(solution)/shard_map/pick/pallas_call | solution.py:47
  8.4 1.9 %cast.1 = (bf16[256,768]{1,0:T(8,128)(2,1)S(1)}, bf16[256,384]{1,0:T(8,128)(2,1)}, bf16[256,384]{1,0:T(8,128)(2,1)}) custom-call(f32[256,768]{1,0:T(8,128)} %bitcast.25), custom_call_target="tpu_custom_call" | custom-call | bytes 1048576 | tf_op jit(solution)/shard_map/cast/pallas_call | solution.py:69
  10.3 2.5 %collective-permute-start.36 = (bf16[256,384]{1,0:T(8,128)(2,1)}, bf16[256,384]{1,0:T(8,128)(2,1)S(1)}, u32[]{:S(2)}, u32[]{:S(2)}) collective-permute-start(bf16[256,384]{1,0:T(8,128)(2,1)} %get-tuple-element.90), channel_id=1, source_target_pairs={{0,12},{4,8},{8,4},{12,0},{1,13},{5,9},{9,5},{13,1},{2,14},{6,10},... | collective-permute-start | bytes 589832 | tf_op jit(solution)/shard_map/ppermute | solution.py:31
  13.6 1.7 %fusion.1 = (f32[512,768]{1,0:T(8,128)S(1)}, bf16[512,768]{1,0:T(8,128)(2,1)}) fusion(bf16[512,768]{1,0:T(8,128)(2,1)S(1)} %copy-done.7, bf16[512,768]{1,0:T(8,128)(2,1)S(1)} %copy-done.8), kind=kLoop, calls=%fused_computation.5 | loop fusion | flops 5505024 | bytes 3932160 | tf_op jit(solution)/shard_map/mul | solution.py:191
  16.1 6.6 %collective-permute-done.34 = bf16[256,384]{1,0:T(8,128)(2,1)S(1)} collective-permute-done((bf16[256,384]{1,0:T(8,128)(2,1)}, bf16[256,384]{1,0:T(8,128)(2,1)S(1)}, u32[]{:S(2)}, u32[]{:S(2)}) %collective-permute-start.34) | collective-permute-done | bytes 196640 | tf_op jit(solution)/shard_map/ppermute | solution.py:31
  25.1 17.6 %conditional.9 = (bf16[256,768]{1,0:T(8,128)(2,1)}) conditional(s32[]{:T(128)} %bitcast.5, bf16[256,768]{1,0:T(8,128)(2,1)S(1)} %get-tuple-element.99, bf16[256,768]{1,0:T(8,128)(2,1)S(1)} %get-tuple-element.99, bf16[256,768]{1,0:T(8,128)(2,1)S(1)} %get-tuple-element.99, ...), branch_computations={%region_15.16_spmd, %region_16.17_spmd, %region_17.18_spmd, %regio... | conditional | bytes 1572912
  25.2 17.5 %collective-permute-done.17 = bf16[256,768]{1,0:T(8,128)(2,1)} collective-permute-done((bf16[256,768]{1,0:T(8,128)(2,1)S(1)}, bf16[256,768]{1,0:T(8,128)(2,1)}, u32[]{:S(2)}, u32[]{:S(2)}) %collective-permute-start.17) | collective-permute-done | bytes 393248 | tf_op jit(solution)/shard_map/cond/branch_2_fun/ppermute | solution.py:37
  44.6 2.6 %collective-permute-start.33 = (bf16[512,384]{1,0:T(8,128)(2,1)S(1)}, bf16[512,384]{1,0:T(8,128)(2,1)}, u32[]{:S(2)}, u32[]{:S(2)}) collective-permute-start(bf16[512,384]{1,0:T(8,128)(2,1)S(1)} %constant_dynamic-update-slice_fusion.pair), channel_id=1, source_target_pairs={{0,12},{4,8},{8,4},{12,0},{1,13},{5,9},{9,5},{13,1},{2,14},{6,10},... | collective-permute-start | bytes 1179656 | tf_op jit(solution)/shard_map/ppermute | solution.py:31
  48.0 10.4 %weight_gradient.1 = (bf16[512,384]{1,0:T(8,128)(2,1)}, bf16[512,384]{1,0:T(8,128)(2,1)}, bf16[512,384]{1,0:T(8,128)(2,1)}, bf16[512,384]{1,0:T(8,128)(2,1)}, bf...) custom-call(s32[8]{0:T(128)} %broadcast_add_fusion.1.order, bf16[512,4096]{1,0:T(8,128)(2,1)} %own_tokens.1, ...), custom_call_target="tpu_custom_call" | custom-call | flops 3221225472 | bytes 9437184 | tf_op jit(solution)/shard_map/weight_gradient/pallas_call | solution.py:107
  58.4 1.4 %collective-permute-start.45 = (bf16[1024,384]{1,0:T(8,128)(2,1)}, bf16[1024,384]{1,0:T(8,128)(2,1)}, u32[]{:S(2)}, u32[]{:S(2)}) collective-permute-start(bf16[1024,384]{1,0:T(8,128)(2,1)} %get-tuple-element.98), channel_id=1, source_target_pairs={{0,2},{2,0},{1,3},{3,1},{4,6},{6,4},{5,7},{7,5},{8,10},{10,8},{9,1... | collective-permute-start | bytes 2359304 | tf_op jit(solution)/shard_map/ppermute | solution.py:27
  59.8 4.2 %collective-permute-done.33.x3 = bf16[512,384]{1,0:T(8,128)(2,1)} collective-permute-done((bf16[512,384]{1,0:T(8,128)(2,1)S(1)}, bf16[512,384]{1,0:T(8,128)(2,1)}, u32[]{:S(2)}, u32[]{:S(2)}) %collective-permute-start.33) | collective-permute-done | bytes 393248 | tf_op jit(solution)/shard_map/ppermute | solution.py:31
  64.0 4.7 %collective-permute-start.42 = (bf16[512,384]{1,0:T(8,128)(2,1)}, bf16[512,384]{1,0:T(8,128)(2,1)}, u32[]{:S(2)}, u32[]{:S(2)}) collective-permute-start(bf16[512,384]{1,0:T(8,128)(2,1)} %get-tuple-element.95), channel_id=1, source_target_pairs={{0,8},{4,12},{8,0},{12,4},{1,9},{5,13},{9,1},{13,5},{2,10},{6,14},... | collective-permute-start | bytes 1179656 | tf_op jit(solution)/shard_map/ppermute | solution.py:31
  68.7 6.4 %pick.2.tokens = bf16[512,2048]{1,0:T(8,128)(2,1)} custom-call(s32[8]{0:T(128)} %broadcast_add_fusion.1.order, bf16[512,4096]{1,0:T(8,128)(2,1)} %own_tokens.1), custom_call_target="tpu_custom_call" | custom-call | bytes 4194304 | tf_op jit(solution)/shard_map/pick/pallas_call | solution.py:47
  76.0 6.5 %up.2 = f32[512,768]{1,0:T(8,128)} custom-call(bf16[512,2048]{1,0:T(8,128)(2,1)} %pick.2.tokens, bf16[512,384]{1,0:T(8,128)(2,1)} %copy-done.5, bf16[512,384]{1,0:T(8,128)(2,1)} %collective-permute-done.31.x1, bf16[512,384]{1,0:T(8,128)(2,1)} %collective-permute-done.32.x2, bf16[512,384]{1,0:T(8,128)(2,1)} %collective-permute-done.33.x3, ...), custom_call_target="tpu_custom_call" | custom-call | flops 1610612736 | bytes 6291456 | tf_op jit(solution)/shard_map/up/pallas_call | solution.py:160
  82.5 6.5 %up.3 = f32[512,768]{1,0:T(8,128)} custom-call(bf16[512,2048]{1,0:T(8,128)(2,1)} %collective-permute-done.38.tokens.other_tokens, bf16[512,384]{1,0:T(8,128)(2,1)} %copy-done.5, bf16[512,384]{1,0:T(8,128)(2,1)} %collective-permute-done.31.x1, bf16[512,384]{1,0:T(8,128)(2,1)} %collective-permute-done.32.x2, bf16[512,384]{1,0:T(8,128)(2,1)} %collective-permute-done.33.x3, ...), custom_call_target="tpu_custom_call" | custom-call | flops 1610612736 | bytes 6291456 | tf_op jit(solution)/shard_map/up/pallas_call | solution.py:160
  89.0 2.0 %collective-permute-start.39 = (f32[512,768]{1,0:T(8,128)}, f32[512,768]{1,0:T(8,128)}, u32[]{:S(2)}, u32[]{:S(2)}) collective-permute-start(f32[512,768]{1,0:T(8,128)} %up.3), channel_id=1, source_target_pairs={{0,1},{1,0},{2,3},{3,2},{4,5},{5,4},{6,7},{7,6},{8,9},{9,8},{10,11... | collective-permute-start | bytes 4718600 | tf_op jit(solution)/shard_map/ppermute | solution.py:27
  95.3 2.6 %collective-permute-start.48 = (bf16[256,384]{1,0:T(8,128)(2,1)S(1)}, bf16[256,384]{1,0:T(8,128)(2,1)S(1)}, u32[]{:S(2)}, u32[]{:S(2)}) collective-permute-start(bf16[256,384]{1,0:T(8,128)(2,1)S(1)} %get-tuple-element.109), channel_id=1, source_target_pairs={{0,12},{4,8},{8,4},{12,0},{1,13},{5,9},{9,5},{13,1},{2,14},{6,10},... | collective-permute-start | bytes 589832 | tf_op jit(solution)/shard_map/ppermute | solution.py:31
  99.0 2.4 %collective-permute-done.46 = bf16[256,384]{1,0:T(8,128)(2,1)S(1)} collective-permute-done((bf16[256,384]{1,0:T(8,128)(2,1)S(1)}, bf16[256,384]{1,0:T(8,128)(2,1)S(1)}, u32[]{:S(2)}, u32[]{:S(2)}) %collective-permute-start.46) | collective-permute-done | bytes 196640 | tf_op jit(solution)/shard_map/ppermute | solution.py:31
  101.4 4.5 %collective-permute-done.48 = bf16[256,384]{1,0:T(8,128)(2,1)S(1)} collective-permute-done((bf16[256,384]{1,0:T(8,128)(2,1)S(1)}, bf16[256,384]{1,0:T(8,128)(2,1)S(1)}, u32[]{:S(2)}, u32[]{:S(2)}) %collective-permute-start.48) | collective-permute-done | bytes 196640 | tf_op jit(solution)/shard_map/ppermute | solution.py:31
  105.9 2.0 %collective-permute-done.47 = bf16[256,384]{1,0:T(8,128)(2,1)S(1)} collective-permute-done((bf16[256,384]{1,0:T(8,128)(2,1)S(1)}, bf16[256,384]{1,0:T(8,128)(2,1)S(1)}, u32[]{:S(2)}, u32[]{:S(2)}) %collective-permute-start.47) | collective-permute-done | bytes 196640 | tf_op jit(solution)/shard_map/ppermute | solution.py:31
  109.0 15.3 %conditional.8 = (bf16[256,768]{1,0:T(8,128)(2,1)}) conditional(s32[]{:T(128)} %bitcast.5, bf16[256,768]{1,0:T(8,128)(2,1)S(1)} %get-tuple-element.100, bf16[256,768]{1,0:T(8,128)(2,1)S(1)} %get-tuple-element.100, bf16[256,768]{1,0:T(8,128)(2,1)S(1)} %get-tuple-element.100, ...), branch_computations={%region_0.1_spmd, %region_1.2_spmd, %region_2.3_spmd, %region_3.4_... | conditional | bytes 1572912
  109.8 14.6 %collective-permute-done.2 = bf16[256,768]{1,0:T(8,128)(2,1)} collective-permute-done((bf16[256,768]{1,0:T(8,128)(2,1)S(1)}, bf16[256,768]{1,0:T(8,128)(2,1)}, u32[]{:S(2)}, u32[]{:S(2)}) %collective-permute-start.2) | collective-permute-done | bytes 393248 | tf_op jit(solution)/shard_map/cond/branch_2_fun/ppermute | solution.py:37
  125.7 2.6 %subtract_bitcast_fusion = (f32[1,256,768]{2,1,0:T(8,128)}, bf16[1,256,768]{2,1,0:T(8,128)(2,1)}) fusion(bf16[256,768]{1,0:T(8,128)(2,1)} %get-tuple-element.112, f32[256,768]{1,0:T(8,128)S(1)} %copy-done.3, bf16[256,768]{1,0:T(8,128)(2,1)} %get-tuple-element.111, bf16[1,256,768]{2,1,0:T(8,128)(2,1)S(1)} %copy-done.13, f32[1,256,768]{2,1,0:T(8,128)S(1)} %copy-done), kind=kLoop, calls=%fused_computation.22 | loop fusion | flops 2949120 | bytes 3932160 | tf_op jit(solution)/shard_map/broadcast_in_dim | solution.py:226
  128.3 2.6 %multiply_convert_fusion = bf16[512,768]{1,0:T(8,128)(2,1)} fusion(f32[512,768]{1,0:T(8,128)S(1)} %get-tuple-element.91, f32[512,768]{1,0:T(8,128)S(1)} %copy-done.1, f32[512,768]{1,0:T(8,128)} %collective-permute-done.39), kind=kLoop, calls=%fused_computation.13 | loop fusion | flops 1179648 | bytes 5505024 | tf_op jit(solution)/shard_map/convert_element_type | solution.py:225
  (77 shorter events, 17.4 us)
Async XLA Ops:
  7.7 40.3 %collective-permute-start.38 = (bf16[512,2048]{1,0:T(8,128)(2,1)}, bf16[512,2048]{1,0:T(8,128)(2,1)}, u32[]{:S(2)}, u32[]{:S(2)}) collective-permute-start(bf16[512,2048]{1,0:T(8,128)(2,1)} %pick.3), channel_id=1, source_target_pairs={{0,1},{1,0},{2,3},{3,2},{4,5},{5,4},{6,7},{7,6},{8,9},{9,8},{10,11... | collective-permute-start | bytes 6291464 | tf_op jit(solution)/shard_map/ppermute | solution.py:27
  10.3 14.8 %copy-start.10 = (bf16[256,768]{1,0:T(8,128)(2,1)}, bf16[256,768]{1,0:T(8,128)(2,1)S(1)}, u32[]{:S(2)}) copy-start(bf16[256,768]{1,0:T(8,128)(2,1)S(1)} %get-tuple-element.99) | copy-start | bytes 1179652
  10.3 13.8 %collective-permute-start.36 = (bf16[256,384]{1,0:T(8,128)(2,1)}, bf16[256,384]{1,0:T(8,128)(2,1)S(1)}, u32[]{:S(2)}, u32[]{:S(2)}) collective-permute-start(bf16[256,384]{1,0:T(8,128)(2,1)} %get-tuple-element.90), channel_id=1, source_target_pairs={{0,12},{4,8},{8,4},{12,0},{1,13},{5,9},{9,5},{13,1},{2,14},{6,10},... | collective-permute-start | bytes 589832 | tf_op jit(solution)/shard_map/ppermute | solution.py:31
  12.8 11.3 %collective-permute-start.35 = (bf16[256,384]{1,0:T(8,128)(2,1)}, bf16[256,384]{1,0:T(8,128)(2,1)S(1)}, u32[]{:S(2)}, u32[]{:S(2)}) collective-permute-start(bf16[256,384]{1,0:T(8,128)(2,1)} %get-tuple-element.90), channel_id=1, source_target_pairs={{0,8},{4,12},{8,0},{12,4},{1,9},{5,13},{9,1},{13,5},{2,10},{6,14},... | collective-permute-start | bytes 589832 | tf_op jit(solution)/shard_map/ppermute | solution.py:31
  13.3 9.4 %collective-permute-start.34 = (bf16[256,384]{1,0:T(8,128)(2,1)}, bf16[256,384]{1,0:T(8,128)(2,1)S(1)}, u32[]{:S(2)}, u32[]{:S(2)}) collective-permute-start(bf16[256,384]{1,0:T(8,128)(2,1)} %get-tuple-element.90), channel_id=1, source_target_pairs={{0,4},{4,0},{8,12},{12,8},{1,5},{5,1},{9,13},{13,9},{2,6},{6,2},{1... | collective-permute-start | bytes 589832 | tf_op jit(solution)/shard_map/ppermute | solution.py:31
  15.2 32.5 %collective-permute-start.40 = (bf16[512,768]{1,0:T(8,128)(2,1)}, bf16[512,768]{1,0:T(8,128)(2,1)}, u32[]{:S(2)}, u32[]{:S(2)}) collective-permute-start(bf16[512,768]{1,0:T(8,128)(2,1)} %get-tuple-element.92.own_grads), channel_id=1, source_target_pairs={{0,1},{1,0},{2,3},{3,2},{4,5},{5,4},{6,7},{7,6},{8,9},{9,8},{10,11... | collective-permute-start | bytes 2359304 | tf_op jit(solution)/shard_map/ppermute | solution.py:27
  22.7 20.9 %collective-permute-start.30 = (bf16[256,384]{1,0:T(8,128)(2,1)}, bf16[256,384]{1,0:T(8,128)(2,1)}, u32[]{:S(2)}, u32[]{:S(2)}) collective-permute-start(bf16[256,384]{1,0:T(8,128)(2,1)} %get-tuple-element.89), channel_id=1, source_target_pairs={{0,2},{2,0},{1,3},{3,1},{4,6},{6,4},{5,7},{7,5},{8,10},{10,8},{9,1... | collective-permute-start | bytes 589832 | tf_op jit(solution)/shard_map/ppermute | solution.py:27
  24.2 34.2 %copy-start.2 = (bf16[1024,384]{1,0:T(8,128)(2,1)}, bf16[1024,384]{1,0:T(8,128)(2,1)S(1)}, u32[]{:S(2)}) copy-start(bf16[1024,384]{1,0:T(8,128)(2,1)S(1)} %constant_dynamic-update-slice_fusion.2.near) | copy-start | bytes 2359300
  24.2 50.9 %collective-permute-start.37 = (bf16[1024,384]{1,0:T(8,128)(2,1)S(1)}, bf16[1024,384]{1,0:T(8,128)(2,1)S(1)}, u32[]{:S(2)}, u32[]{:S(2)}) collective-permute-start(bf16[1024,384]{1,0:T(8,128)(2,1)S(1)} %constant_dynamic-update-slice_fusion.2.near), channel_id=1, source_target_pairs={{0,2},{2,0},{1,3},{3,1},{4,6},{6,4},{5,7},{7,5},{8,10},{10,8},{9,1... | collective-permute-start | bytes 2359304 | tf_op jit(solution)/shard_map/ppermute | solution.py:27
  25.1 17.6 %collective-permute-start.17 = (bf16[256,768]{1,0:T(8,128)(2,1)S(1)}, bf16[256,768]{1,0:T(8,128)(2,1)}, u32[]{:S(2)}, u32[]{:S(2)}) collective-permute-start(bf16[256,768]{1,0:T(8,128)(2,1)S(1)} %param.17), channel_id=1, source_target_pairs={{0,48},{16,32},{32,16},{48,0},{64,112},{80,96},{96,80},{112,64},{1... | collective-permute-start | bytes 1179656 | tf_op jit(solution)/shard_map/cond/branch_2_fun/ppermute | solution.py:37
  44.6 13.7 %copy-start.5 = (bf16[512,384]{1,0:T(8,128)(2,1)}, bf16[512,384]{1,0:T(8,128)(2,1)S(1)}, u32[]{:S(2)}) copy-start(bf16[512,384]{1,0:T(8,128)(2,1)S(1)} %constant_dynamic-update-slice_fusion.pair) | copy-start | bytes 1179652
  44.6 19.3 %collective-permute-start.33 = (bf16[512,384]{1,0:T(8,128)(2,1)S(1)}, bf16[512,384]{1,0:T(8,128)(2,1)}, u32[]{:S(2)}, u32[]{:S(2)}) collective-permute-start(bf16[512,384]{1,0:T(8,128)(2,1)S(1)} %constant_dynamic-update-slice_fusion.pair), channel_id=1, source_target_pairs={{0,12},{4,8},{8,4},{12,0},{1,13},{5,9},{9,5},{13,1},{2,14},{6,10},... | collective-permute-start | bytes 1179656 | tf_op jit(solution)/shard_map/ppermute | solution.py:31
  47.2 16.8 %collective-permute-start.32 = (bf16[512,384]{1,0:T(8,128)(2,1)S(1)}, bf16[512,384]{1,0:T(8,128)(2,1)}, u32[]{:S(2)}, u32[]{:S(2)}) collective-permute-start(bf16[512,384]{1,0:T(8,128)(2,1)S(1)} %constant_dynamic-update-slice_fusion.pair), channel_id=1, source_target_pairs={{0,8},{4,12},{8,0},{12,4},{1,9},{5,13},{9,1},{13,5},{2,10},{6,14},... | collective-permute-start | bytes 1179656 | tf_op jit(solution)/shard_map/ppermute | solution.py:31
  47.7 21.0 %collective-permute-start.31 = (bf16[512,384]{1,0:T(8,128)(2,1)S(1)}, bf16[512,384]{1,0:T(8,128)(2,1)}, u32[]{:S(2)}, u32[]{:S(2)}) collective-permute-start(bf16[512,384]{1,0:T(8,128)(2,1)S(1)} %constant_dynamic-update-slice_fusion.pair), channel_id=1, source_target_pairs={{0,4},{4,0},{8,12},{12,8},{1,5},{5,1},{9,13},{13,9},{2,6},{6,2},{1... | collective-permute-start | bytes 1179656 | tf_op jit(solution)/shard_map/ppermute | solution.py:31
  58.4 35.4 %collective-permute-start.45 = (bf16[1024,384]{1,0:T(8,128)(2,1)}, bf16[1024,384]{1,0:T(8,128)(2,1)}, u32[]{:S(2)}, u32[]{:S(2)}) collective-permute-start(bf16[1024,384]{1,0:T(8,128)(2,1)} %get-tuple-element.98), channel_id=1, source_target_pairs={{0,2},{2,0},{1,3},{3,1},{4,6},{6,4},{5,7},{7,5},{8,10},{10,8},{9,1... | collective-permute-start | bytes 2359304 | tf_op jit(solution)/shard_map/ppermute | solution.py:27
  64.0 27.1 %collective-permute-start.41 = (bf16[512,384]{1,0:T(8,128)(2,1)}, bf16[512,384]{1,0:T(8,128)(2,1)}, u32[]{:S(2)}, u32[]{:S(2)}) collective-permute-start(bf16[512,384]{1,0:T(8,128)(2,1)} %get-tuple-element.94), channel_id=1, source_target_pairs={{0,4},{4,0},{8,12},{12,8},{1,5},{5,1},{9,13},{13,9},{2,6},{6,2},{1... | collective-permute-start | bytes 1179656 | tf_op jit(solution)/shard_map/ppermute | solution.py:31
  64.0 27.1 %collective-permute-start.42 = (bf16[512,384]{1,0:T(8,128)(2,1)}, bf16[512,384]{1,0:T(8,128)(2,1)}, u32[]{:S(2)}, u32[]{:S(2)}) collective-permute-start(bf16[512,384]{1,0:T(8,128)(2,1)} %get-tuple-element.95), channel_id=1, source_target_pairs={{0,8},{4,12},{8,0},{12,4},{1,9},{5,13},{9,1},{13,5},{2,10},{6,14},... | collective-permute-start | bytes 1179656 | tf_op jit(solution)/shard_map/ppermute | solution.py:31
  68.7 22.4 %collective-permute-start.43 = (bf16[512,384]{1,0:T(8,128)(2,1)}, bf16[512,384]{1,0:T(8,128)(2,1)S(1)}, u32[]{:S(2)}, u32[]{:S(2)}) collective-permute-start(bf16[512,384]{1,0:T(8,128)(2,1)} %get-tuple-element.96), channel_id=1, source_target_pairs={{0,12},{4,8},{8,4},{12,0},{1,13},{5,9},{9,5},{13,1},{2,14},{6,10},... | collective-permute-start | bytes 1179656 | tf_op jit(solution)/shard_map/ppermute | solution.py:31
  89.0 39.3 %collective-permute-start.39 = (f32[512,768]{1,0:T(8,128)}, f32[512,768]{1,0:T(8,128)}, u32[]{:S(2)}, u32[]{:S(2)}) collective-permute-start(f32[512,768]{1,0:T(8,128)} %up.3), channel_id=1, source_target_pairs={{0,1},{1,0},{2,3},{3,2},{4,5},{5,4},{6,7},{7,6},{8,9},{9,8},{10,11... | collective-permute-start | bytes 4718600 | tf_op jit(solution)/shard_map/ppermute | solution.py:27
  92.4 6.6 %collective-permute-start.44 = (bf16[256,384]{1,0:T(8,128)(2,1)S(1)}, bf16[256,384]{1,0:T(8,128)(2,1)S(1)}, u32[]{:S(2)}, u32[]{:S(2)}) collective-permute-start(bf16[256,384]{1,0:T(8,128)(2,1)S(1)} %slice.49), channel_id=1, source_target_pairs={{0,2},{2,0},{1,3},{3,1},{4,6},{6,4},{5,7},{7,5},{8,10},{10,8},{9,1... | collective-permute-start | bytes 589832 | tf_op jit(solution)/shard_map/ppermute | solution.py:27
  95.2 6.2 %collective-permute-start.46 = (bf16[256,384]{1,0:T(8,128)(2,1)S(1)}, bf16[256,384]{1,0:T(8,128)(2,1)S(1)}, u32[]{:S(2)}, u32[]{:S(2)}) collective-permute-start(bf16[256,384]{1,0:T(8,128)(2,1)S(1)} %get-tuple-element.108), channel_id=1, source_target_pairs={{0,4},{4,0},{8,12},{12,8},{1,5},{5,1},{9,13},{13,9},{2,6},{6,2},{1... | collective-permute-start | bytes 589832 | tf_op jit(solution)/shard_map/ppermute | solution.py:31
  95.3 10.5 %collective-permute-start.48 = (bf16[256,384]{1,0:T(8,128)(2,1)S(1)}, bf16[256,384]{1,0:T(8,128)(2,1)S(1)}, u32[]{:S(2)}, u32[]{:S(2)}) collective-permute-start(bf16[256,384]{1,0:T(8,128)(2,1)S(1)} %get-tuple-element.109), channel_id=1, source_target_pairs={{0,12},{4,8},{8,4},{12,0},{1,13},{5,9},{9,5},{13,1},{2,14},{6,10},... | collective-permute-start | bytes 589832 | tf_op jit(solution)/shard_map/ppermute | solution.py:31
  97.9 9.9 %collective-permute-start.47 = (bf16[256,384]{1,0:T(8,128)(2,1)S(1)}, bf16[256,384]{1,0:T(8,128)(2,1)S(1)}, u32[]{:S(2)}, u32[]{:S(2)}) collective-permute-start(bf16[256,384]{1,0:T(8,128)(2,1)S(1)} %get-tuple-element.110), channel_id=1, source_target_pairs={{0,8},{4,12},{8,0},{12,4},{1,9},{5,13},{9,1},{13,5},{2,10},{6,14},... | collective-permute-start | bytes 589832 | tf_op jit(solution)/shard_map/ppermute | solution.py:31
  109.0 15.3 %collective-permute-start.2 = (bf16[256,768]{1,0:T(8,128)(2,1)S(1)}, bf16[256,768]{1,0:T(8,128)(2,1)}, u32[]{:S(2)}, u32[]{:S(2)}) collective-permute-start(bf16[256,768]{1,0:T(8,128)(2,1)S(1)} %param.2), channel_id=1, source_target_pairs={{0,48},{16,32},{32,16},{48,0},{64,112},{80,96},{96,80},{112,64},{1... | collective-permute-start | bytes 1179656 | tf_op jit(solution)/shard_map/cond/branch_2_fun/ppermute | solution.py:37
  (13 other events, 98.2 us)
where the time goes:
time: 132 us; the launch traced here: 131 us
  waiting for transfers between devices  51.7 us (39%)
  Pallas kernels  38.3 us (29%)
  starting transfers between devices  23.7 us (18%)
  other arithmetic  12.7 us (10%)
  local copies, waits for them, and re-layouts  3.56 us (3%)
    ppermute x2, waiting for transfers between devices, branch(): return lambda value: lax.ppermute(value, ('yh', 'z'), route)  32.1 us
    ppermute x12, waiting for transfers between devices, swap_x(): return lax.ppermute(block, 'x', [(i, i ^ distance) for i in range(4)])  19.7 us
    ppermute x12, starting transfers between devices, swap_x(): return lax.ppermute(block, 'x', [(i, i ^ distance) for i in range(4)])  15 us
    pallas_call x2, Pallas kernels, up_partial(): pl.pallas_call(up_kernel, out_shape=SHAPE((ROWS, COLS), F32), in_specs=[W...  13 us
    pallas_call x2, Pallas kernels, pick(): pl.pallas_call(pick_kernel, out_shape=SHAPE((ROWS, 8 * BLOCK), BF16), gri...  13 us
    pallas_call x1, Pallas kernels, partial_gradient(): pl.pallas_call(grad_kernel, out_shape=[SHAPE((2 * BLOCK, HALF), BF16)] *...  10.4 us
    ppermute x7, starting transfers between devices, swap(): return lax.ppermute(block, axis, [(0, 1), (1, 0)])  7.86 us
  transfers between devices with their start and end apart: 21, of which 7 were waited for; matrix products, arithmetic and copies ran while one was open for 9% of the time, Pallas kernels for 24%

commit v1 on v0

v1 whole, which is shorter than its diff:
```python
import jax
import jax.numpy as jnp
from jax import lax
from jax.experimental import pallas as pl
from jax.experimental.pallas import tpu as pltpu
from jax.sharding import Mesh, PartitionSpec as P


D = 4096
COLS = 768
HALF = COLS // 2
BLOCK = 256
ROWS = 512

inner_beta = 0.9
inner_rate = 0.5
outer_mu = 0.9
outer_rate = 0.7

F32 = jnp.float32
BF16 = jnp.bfloat16
SHAPE = jax.ShapeDtypeStruct
WHOLE = pl.BlockSpec(memory_space=pltpu.VMEM)


def swap(block, axis):
    return lax.ppermute(block, axis, [(0, 1), (1, 0)])


def swap_x(block, distance):
    return lax.ppermute(block, "x", [(i, i ^ distance) for i in range(4)])


def pair_exchange(block, partner_xor):
    def branch(distance):
        route = [(i, i ^ distance) for i in range(16)]
        return lambda value: lax.ppermute(value, ("yh", "z"), route)

    return lax.switch(partner_xor - 1, [branch(d) for d in range(1, 16)], block)


def limits(mebibytes):
    return pltpu.CompilerParams(vmem_limit_bytes=mebibytes * 2**20)


def pick_kernel(tokens, other, own, sems):
    core = lax.axis_index("core")
    copies = []
    for which, (side, out) in enumerate(((1 - core, other), (core, own))):
        for step in range(8):
            x = lax.axis_index("x") ^ (step // 2)
            y = lax.axis_index("yl") ^ (step % 2)
            owner = (x * 2 + y) * 2 + side
            columns = pl.ds(pl.multiple_of(owner * BLOCK, BLOCK), BLOCK)
            copies.append(
                pltpu.make_async_copy(
                    tokens.at[:, columns],
                    out.at[:, step * BLOCK : (step + 1) * BLOCK],
                    sems.at[which, step],
                )
            )
    for copy in copies:
        copy.start()
    for copy in copies:
        copy.wait()


def pick(tokens):
    return pl.pallas_call(
        pick_kernel,
        out_shape=[SHAPE((ROWS, 8 * BLOCK), BF16)] * 2,
        in_specs=[pl.BlockSpec(memory_space=pl.ANY)],
        out_specs=[WHOLE] * 2,
        scratch_shapes=[pltpu.SemaphoreType.DMA((2, 8))],
        cost_estimate=pl.CostEstimate(flops=0, bytes_accessed=2**22, transcendentals=0),
        compiler_params=limits(58),
        name="pick",
    )(tokens)


def cast_kernel(slow, whole, first, second):
    fast = slow[...].astype(BF16)
    whole[...] = fast
    first[...] = fast[:, :HALF]
    second[...] = fast[:, HALF:]


def cast(slow):
    return pl.pallas_call(
        cast_kernel,
        out_shape=[SHAPE((BLOCK, COLS), BF16)] + [SHAPE((BLOCK, HALF), BF16)] * 2,
        in_specs=[WHOLE],
        out_specs=[WHOLE] * 3,
        cost_estimate=pl.CostEstimate(flops=0, bytes_accessed=2**20, transcendentals=0),
        compiler_params=limits(4),
        name="cast",
    )(slow)


def join_kernel(*refs):
    out = refs[-1]
    for place, part in enumerate(refs[:-1]):
        out[place * BLOCK : (place + 1) * BLOCK, :] = part[...]


def join(*parts):
    return pl.pallas_call(
        join_kernel,
        out_shape=SHAPE((len(parts) * BLOCK, HALF), BF16),
        in_specs=[WHOLE] * len(parts),
        out_specs=WHOLE,
        cost_estimate=pl.CostEstimate(flops=0, bytes_accessed=2**20, transcendentals=0),
        compiler_params=limits(4),
        name="join",
    )(*parts)


def grad_kernel(own_tokens, other_tokens, own_grads, other_grads, a0, a1, a2, a3, keep, send):
    contract = (((0,), (0,)), ((), ()))
    for step in range(8):
        distance, side = divmod(step, 2)
        columns = slice(step * BLOCK, (step + 1) * BLOCK)
        total = lax.dot_general(
            own_tokens[:, columns], own_grads[...], contract, preferred_element_type=F32
        ) + lax.dot_general(
            other_tokens[:, columns], other_grads[...], contract, preferred_element_type=F32
        )
        total = total.astype(BF16)
        (a0, a1, a2, a3)[distance][side * BLOCK : (side + 1) * BLOCK, :] = total[:, :HALF]
        (keep, send)[side][distance * BLOCK : (distance + 1) * BLOCK, :] = total[:, HALF:]


def partial_gradient(own_tokens, other_tokens, own_grads, other_grads):
    return pl.pallas_call(
        grad_kernel,
        out_shape=[SHAPE((2 * BLOCK, HALF), BF16)] * 4 + [SHAPE((4 * BLOCK, HALF), BF16)] * 2,
        in_specs=[WHOLE] * 4,
        out_specs=[WHOLE] * 6,
        cost_estimate=pl.CostEstimate(
            flops=2 * 1024 * 2048 * 768, bytes_accessed=9 * 2**20, transcendentals=0
        ),
        compiler_params=limits(14),
        name="weight_gradient",
    )(own_tokens, other_tokens, own_grads, other_grads)


def up_kernel(tokens, pair, x1, x2, x3, near, far, out):
    rows = 128

    @pl.loop(0, ROWS // rows)
    def _(tile):
        here = pl.ds(pl.multiple_of(tile * rows, rows), rows)

        def times(step, count, weight):
            return jnp.dot(
                tokens[here, step * BLOCK : (step + count) * BLOCK],
                weight,
                preferred_element_type=F32,
            )

        total = jnp.zeros((rows, HALF), F32)
        for distance, weight in enumerate((pair, x1, x2, x3)):
            total += times(2 * distance, 2, weight[...])
        out[here, :HALF] = total
        total = jnp.zeros((rows, HALF), F32)
        for side, weight in enumerate((near, far)):
            for distance in range(4):
                total += times(
                    2 * distance + side, 1, weight[distance * BLOCK : (distance + 1) * BLOCK, :]
                )
        out[here, HALF:] = total


def up_partial(tokens, *weights):
    return pl.pallas_call(
        up_kernel,
        out_shape=SHAPE((ROWS, COLS), F32),
        in_specs=[WHOLE] * 7,
        out_specs=WHOLE,
        cost_estimate=pl.CostEstimate(
            flops=2 * 512 * 2048 * 768, bytes_accessed=6 * 2**20, transcendentals=0
        ),
        compiler_params=limits(12),
        name="up",
    )(tokens, *weights)


def inner_kernel(part_a, part_b, got_a, b1, b2, b3, inner_mom, slow, fast, inner_new, outer_grad):
    scale = float(D) ** (-0.5)
    total_b = part_b[...]
    for got in (b1, b2, b3):
        total_b += got[...].astype(F32)
    for here, total in (
        (slice(0, HALF), part_a[...] + got_a[...].astype(F32)),
        (slice(HALF, COLS), total_b),
    ):
        inner = (inner_beta * inner_mom[:, here].astype(F32) + total * scale).astype(BF16)
        inner_new[:, here] = inner
        outer_grad[:, here] = (
            slow[:, here] - (fast[:, here].astype(F32) - inner_rate * inner.astype(F32))
        ).astype(BF16)


def inner_update(*operands):
    return pl.pallas_call(
        inner_kernel,
        out_shape=[SHAPE((BLOCK, COLS), BF16)] * 2,
        in_specs=[WHOLE] * 9,
        out_specs=[WHOLE] * 2,
        cost_estimate=pl.CostEstimate(flops=0, bytes_accessed=2**21, transcendentals=0),
        compiler_params=limits(8),
        name="inner",
    )(*operands)


def outer_kernel(slow, fast, inner_new, slow_partner, grad_partner, outer_mom, outer_new, slow_new):
    slow_values = slow[...]
    outer_grad = slow_values - (
        fast[...].astype(F32) - inner_rate * inner_new[...].astype(F32)
    )
    mean_slow = 0.5 * (slow_values + slow_partner[...].astype(F32))
    mean_grad = 0.5 * (outer_grad + grad_partner[...].astype(F32))
    outer = (outer_mu * outer_mom[...].astype(F32) + mean_grad).astype(BF16)
    outer_new[...] = outer
    slow_new[...] = mean_slow - outer_rate * (mean_grad + outer_mu * outer.astype(F32))


def outer_update(*operands):
    return pl.pallas_call(
        outer_kernel,
        out_shape=[SHAPE((BLOCK, COLS), BF16), SHAPE((BLOCK, COLS), F32)],
        in_specs=[WHOLE] * 6,
        out_specs=[WHOLE] * 2,
        cost_estimate=pl.CostEstimate(flops=0, bytes_accessed=2**21, transcendentals=0),
        compiler_params=limits(8),
        name="outer",
    )(*operands)


def local(tokens, gate_pre, upstream, slow, inner_mom, outer_mom, pairing):
    weight_scale = float(D) ** (-0.5)
    slow_shard = slow[0]
    fast_weight, weight_a, weight_b = cast(slow_shard)
    partner_xor = pairing[0]

    other_tokens, own_tokens = pick(tokens)
    other_tokens = swap(other_tokens, "core")

    gate_values = gate_pre.astype(F32)
    sigmoid_gate = jax.nn.sigmoid(gate_values)
    upstream_values = upstream.astype(F32)
    grad_rows = (upstream_values * gate_values * sigmoid_gate).astype(BF16)
    factor = (
        upstream_values * sigmoid_gate * (1.0 + gate_values * (1.0 - sigmoid_gate)) * weight_scale
    )
    grad_rows, factor = lax.optimization_barrier((grad_rows, factor))
    other_grads = swap(grad_rows, "core")

    pair = join(weight_a, swap(weight_a, "yl"))
    near = join(weight_b, *[swap_x(weight_b, k) for k in (1, 2, 3)])
    weights = [pair] + [swap_x(pair, k) for k in (1, 2, 3)] + [near, swap(near, "yl")]

    a0, a1, a2, a3, keep, send = partial_gradient(
        own_tokens, other_tokens, grad_rows, other_grads
    )
    part_a = a0.astype(F32)
    for k, piece in ((1, a1), (2, a2), (3, a3)):
        part_a = part_a + swap_x(piece, k).astype(F32)
    got_a = swap(part_a[BLOCK:].astype(BF16), "yl")
    part_b = keep.astype(F32) + swap(send, "yl").astype(F32)
    part_b = part_b.reshape(4, BLOCK, HALF)
    got_b = [swap_x(part_b[k].astype(BF16), k) for k in (1, 2, 3)]
    inner_new, outer_grad = inner_update(
        part_a[:BLOCK], part_b[0], got_a, *got_b, inner_mom[0], slow_shard, fast_weight
    )
    slow_partner = pair_exchange(fast_weight, partner_xor)
    grad_partner = pair_exchange(outer_grad, partner_xor)
    outer_new, slow_new = outer_update(
        slow_shard, fast_weight, inner_new, slow_partner, grad_partner, outer_mom[0]
    )

    other_up = up_partial(other_tokens, *weights)
    own_up = up_partial(own_tokens, *weights)
    other_up = swap(other_up, "core")
    gate_grad = ((own_up + other_up) * factor).astype(BF16)
    return (gate_grad, inner_new[None], outer_new[None], slow_new[None])


def solution(mesh):
    fine = Mesh(mesh.devices.reshape(2, 8, 4, 2, 2), ("yh", "z", "x", "yl", "core"))
    rep, fsdp = ("yh", "z"), ("x", "yl", "core")
    rows = P(rep + fsdp, None)
    state = P(rep, fsdp, None)


    return jax.shard_map(
        local,
        mesh=fine,
        in_specs=(rows, rows, rows, state, state, state, P()),
        out_specs=(rows, state, state, state),
        check_vma=False,
    )
```

time: 132 us -> 138 us (1.045)
  the two profiles are of different devices: /device:TPU:65 before, /device:TPU:32 now
where the time goes in v1:
time: 138 us; the launch traced here: 137 us
  waiting for transfers between devices  81.9 us (59%)
  starting transfers between devices  25.7 us (19%)
  Pallas kernels  19.7 us (14%)
  other arithmetic  6.28 us (5%)
  local copies, waits for them, and re-layouts  2.72 us (2%)
    ppermute x12, waiting for transfers between devices, swap_x(): return lax.ppermute(block, 'x', [(i, i ^ distance) for i in range(4)])  54.4 us
    ppermute x2, waiting for transfers between devices, branch(): return lambda value: lax.ppermute(value, ('yh', 'z'), route)  27.6 us
    ppermute x12, starting transfers between devices, swap_x(): return lax.ppermute(block, 'x', [(i, i ^ distance) for i in range(4)])  16.7 us
    pallas_call x2, Pallas kernels, up_partial(): pl.pallas_call(up_kernel, out_shape=SHAPE((ROWS, COLS), F32), in_specs=[W...  6.95 us
    ppermute x7, starting transfers between devices, swap(): return lax.ppermute(block, axis, [(0, 1), (1, 0)])  5.54 us
    pallas_call x1, Pallas kernels, pick(): pl.pallas_call(pick_kernel, out_shape=[SHAPE((ROWS, 8 * BLOCK), BF16)] *...  4.45 us
    pallas_call x1, Pallas kernels, partial_gradient(): pl.pallas_call(grad_kernel, out_shape=[SHAPE((2 * BLOCK, HALF), BF16)] *...  4.41 us
    ppermute x2, starting transfers between devices, branch(): return lambda value: lax.ppermute(value, ('yh', 'z'), route)  3.38 us
  transfers between devices with their start and end apart: 21, of which 13 were waited for; matrix products, arithmetic and copies ran while one was open for 3% of the time, Pallas kernels for 11%

profile of v1, /device:TPU:32, one launch (start us, length us, event | category | flops | bytes accessed | tf_op | source)
XLA Modules:
  0.0 137.3 jit_solution(10916052311659129869)
XLA Ops:
  0.6 4.4 %pick.1 = (bf16[512,2048]{1,0:T(8,128)(2,1)}, bf16[512,2048]{1,0:T(8,128)(2,1)}) custom-call(bf16[512,4096]{1,0:T(8,128)(2,1)} %tokens.1), custom_call_target="tpu_custom_call" | custom-call | bytes 4194304 | tf_op jit(solution)/shard_map/pick/pallas_call | solution.py:69
  6.9 2.7 %collective-permute-start.35 = (bf16[256,384]{1,0:T(8,128)(2,1)S(1)}, bf16[256,384]{1,0:T(8,128)(2,1)S(1)}, u32[]{:S(2)}, u32[]{:S(2)}) collective-permute-start(bf16[256,384]{1,0:T(8,128)(2,1)S(1)} %get-tuple-element.85.refs_0_), channel_id=1, source_target_pairs={{0,8},{4,12},{8,0},{12,4},{1,9},{5,13},{9,1},{13,5},{2,10},{6,14},... | collective-permute-start | bytes 589832 | tf_op jit(solution)/shard_map/ppermute | solution.py:31
  13.2 6.0 %collective-permute-done.35.refs_2_ = bf16[256,384]{1,0:T(8,128)(2,1)S(1)} collective-permute-done((bf16[256,384]{1,0:T(8,128)(2,1)S(1)}, bf16[256,384]{1,0:T(8,128)(2,1)S(1)}, u32[]{:S(2)}, u32[]{:S(2)}) %collective-permute-start.35) | collective-permute-done | bytes 196640 | tf_op jit(solution)/shard_map/ppermute | solution.py:31
  19.2 2.6 %collective-permute-done.36.refs_3_ = bf16[256,384]{1,0:T(8,128)(2,1)S(1)} collective-permute-done((bf16[256,384]{1,0:T(8,128)(2,1)S(1)}, bf16[256,384]{1,0:T(8,128)(2,1)S(1)}, u32[]{:S(2)}, u32[]{:S(2)}) %collective-permute-start.36) | collective-permute-done | bytes 196640 | tf_op jit(solution)/shard_map/ppermute | solution.py:31
  27.5 8.1 %collective-permute-done.31.x1 = bf16[512,384]{1,0:T(8,128)(2,1)S(1)} collective-permute-done((bf16[512,384]{1,0:T(8,128)(2,1)S(1)}, bf16[512,384]{1,0:T(8,128)(2,1)S(1)}, u32[]{:S(2)}, u32[]{:S(2)}) %collective-permute-start.31) | collective-permute-done | bytes 393248 | tf_op jit(solution)/shard_map/ppermute | solution.py:31
  36.1 5.8 %collective-permute-done.32.x2 = bf16[512,384]{1,0:T(8,128)(2,1)S(1)} collective-permute-done((bf16[512,384]{1,0:T(8,128)(2,1)S(1)}, bf16[512,384]{1,0:T(8,128)(2,1)S(1)}, u32[]{:S(2)}, u32[]{:S(2)}) %collective-permute-start.32) | collective-permute-done | bytes 393248 | tf_op jit(solution)/shard_map/ppermute | solution.py:31
  41.9 8.1 %collective-permute-done.33.x3 = bf16[512,384]{1,0:T(8,128)(2,1)S(1)} collective-permute-done((bf16[512,384]{1,0:T(8,128)(2,1)S(1)}, bf16[512,384]{1,0:T(8,128)(2,1)S(1)}, u32[]{:S(2)}, u32[]{:S(2)}) %collective-permute-start.33) | collective-permute-done | bytes 393248 | tf_op jit(solution)/shard_map/ppermute | solution.py:31
  50.0 4.1 %up.3 = f32[512,768]{1,0:T(8,128)} custom-call(bf16[512,2048]{1,0:T(8,128)(2,1)S(1)} %collective-permute-done.38.tokens.other_tokens, bf16[512,384]{1,0:T(8,128)(2,1)S(1)} %join.2.pair, bf16[512,384]{1,0:T(8,128)(2,1)S(1)} %collective-permute-done.31.x1, bf16[512,384]{1,0:T(8,128)(2,1)S(1)} %collective-permute-done.32.x2, ...), custom_call_target="tpu_custom_call" | custom-call | flops 1610612736 | bytes 6291456 | tf_op jit(solution)/shard_map/up/pallas_call | solution.py:175
  54.2 4.4 %weight_gradient.1 = (bf16[512,384]{1,0:T(8,128)(2,1)S(1)}, bf16[512,384]{1,0:T(8,128)(2,1)S(1)}, bf16[512,384]{1,0:T(8,128)(2,1)S(1)}, bf16[512,384]{1,0:T(8,12...) custom-call(bf16[512,2048]{1,0:T(8,128)(2,1)S(1)} %copy-done.3, ...), custom_call_target="tpu_custom_call" | custom-call | flops 3221225472 | bytes 9437184 | tf_op jit(solution)/shard_map/weight_gradient/pallas_call | solution.py:134
  60.7 20.0 %conditional.2 = (bf16[256,768]{1,0:T(8,128)(2,1)}) conditional(s32[]{:T(128)} %bitcast.3, bf16[256,768]{1,0:T(8,128)(2,1)S(1)} %get-tuple-element.95.fast, bf16[256,768]{1,0:T(8,128)(2,1)S(1)} %get-tuple-element.95.fast, bf16[256,768]{1,0:T(8,128)(2,1)S(1)} %get-tuple-element.95.fast, ...), branch_computations={%region_0.0_spmd, %region_1.0_spmd, %region_2.0_spmd, %region_3.0_... | conditional | bytes 1572912 | solution.py:39
  60.7 2.0 %collective-permute-start.2 = (bf16[256,768]{1,0:T(8,128)(2,1)S(1)}, bf16[256,768]{1,0:T(8,128)(2,1)}, u32[]{:S(2)}, u32[]{:S(2)}) collective-permute-start(bf16[256,768]{1,0:T(8,128)(2,1)S(1)} %param.2), channel_id=1, source_target_pairs={{0,48},{16,32},{32,16},{48,0},{64,112},{80,96},{96,80},{112,64},{1... | collective-permute-start | bytes 1179656 | tf_op jit(solution)/shard_map/cond/branch_2_fun/ppermute | solution.py:37
  62.7 18.0 %collective-permute-done.2 = bf16[256,768]{1,0:T(8,128)(2,1)} collective-permute-done((bf16[256,768]{1,0:T(8,128)(2,1)S(1)}, bf16[256,768]{1,0:T(8,128)(2,1)}, u32[]{:S(2)}, u32[]{:S(2)}) %collective-permute-start.2) | collective-permute-done | bytes 393248 | tf_op jit(solution)/shard_map/cond/branch_2_fun/ppermute | solution.py:37
  80.7 3.1 %collective-permute-start.42 = (bf16[512,384]{1,0:T(8,128)(2,1)}, bf16[512,384]{1,0:T(8,128)(2,1)S(1)}, u32[]{:S(2)}, u32[]{:S(2)}) collective-permute-start(bf16[512,384]{1,0:T(8,128)(2,1)} %copy-done.14), channel_id=1, source_target_pairs={{0,8},{4,12},{8,0},{12,4},{1,9},{5,13},{9,1},{13,5},{2,10},{6,14},... | collective-permute-start | bytes 1179656 | tf_op jit(solution)/shard_map/ppermute | solution.py:31
  85.4 7.5 %collective-permute-done.41 = bf16[512,384]{1,0:T(8,128)(2,1)S(1)} collective-permute-done((bf16[512,384]{1,0:T(8,128)(2,1)}, bf16[512,384]{1,0:T(8,128)(2,1)S(1)}, u32[]{:S(2)}, u32[]{:S(2)}) %collective-permute-start.41) | collective-permute-done | bytes 393248 | tf_op jit(solution)/shard_map/ppermute | solution.py:31
  92.9 8.1 %collective-permute-done.42 = bf16[512,384]{1,0:T(8,128)(2,1)S(1)} collective-permute-done((bf16[512,384]{1,0:T(8,128)(2,1)}, bf16[512,384]{1,0:T(8,128)(2,1)S(1)}, u32[]{:S(2)}, u32[]{:S(2)}) %collective-permute-start.42) | collective-permute-done | bytes 393248 | tf_op jit(solution)/shard_map/ppermute | solution.py:31
  101.0 2.4 %collective-permute-done.43 = bf16[512,384]{1,0:T(8,128)(2,1)S(1)} collective-permute-done((bf16[512,384]{1,0:T(8,128)(2,1)S(1)}, bf16[512,384]{1,0:T(8,128)(2,1)S(1)}, u32[]{:S(2)}, u32[]{:S(2)}) %collective-permute-start.43) | collective-permute-done | bytes 393248 | tf_op jit(solution)/shard_map/ppermute | solution.py:31
  107.0 3.1 %collective-permute-start.47 = (bf16[256,384]{1,0:T(8,128)(2,1)S(1)}, bf16[256,384]{1,0:T(8,128)(2,1)S(1)}, u32[]{:S(2)}, u32[]{:S(2)}) collective-permute-start(bf16[256,384]{1,0:T(8,128)(2,1)S(1)} %get-tuple-element.105), channel_id=1, source_target_pairs={{0,8},{4,12},{8,0},{12,4},{1,9},{5,13},{9,1},{13,5},{2,10},{6,14},... | collective-permute-start | bytes 589832 | tf_op jit(solution)/shard_map/ppermute | solution.py:31
  111.7 2.9 %up.2 = f32[512,768]{1,0:T(8,128)S(1)} custom-call(bf16[512,2048]{1,0:T(8,128)(2,1)S(1)} %copy-done.4, bf16[512,384]{1,0:T(8,128)(2,1)S(1)} %join.2.pair, bf16[512,384]{1,0:T(8,128)(2,1)S(1)} %copy-done.6, bf16[512,384]{1,0:T(8,128)(2,1)S(1)} %copy-done.8, bf16[512,384]{1,0:T(8,128)(2,1)S(1)} %copy-done.10, bf16[1024,384]{1,0:T(8,128)(2,1)S(1)} %join.3.near, ...), custom_call_target="tpu_custom_call" | custom-call | flops 1610612736 | bytes 6291456 | tf_op jit(solution)/shard_map/up/pallas_call | solution.py:175
  114.7 2.2 %collective-permute-done.47.b2 = bf16[256,384]{1,0:T(8,128)(2,1)S(1)} collective-permute-done((bf16[256,384]{1,0:T(8,128)(2,1)S(1)}, bf16[256,384]{1,0:T(8,128)(2,1)S(1)}, u32[]{:S(2)}, u32[]{:S(2)}) %collective-permute-start.47) | collective-permute-done | bytes 196640 | tf_op jit(solution)/shard_map/ppermute | solution.py:31
  116.9 2.1 %collective-permute-done.48.b3 = bf16[256,384]{1,0:T(8,128)(2,1)S(1)} collective-permute-done((bf16[256,384]{1,0:T(8,128)(2,1)S(1)}, bf16[256,384]{1,0:T(8,128)(2,1)S(1)}, u32[]{:S(2)}, u32[]{:S(2)}) %collective-permute-start.48) | collective-permute-done | bytes 196640 | tf_op jit(solution)/shard_map/ppermute | solution.py:31
  120.0 10.9 %conditional.3 = (bf16[256,768]{1,0:T(8,128)(2,1)}) conditional(s32[]{:T(128)} %bitcast.3, bf16[256,768]{1,0:T(8,128)(2,1)S(1)} %get-tuple-element.97, bf16[256,768]{1,0:T(8,128)(2,1)S(1)} %get-tuple-element.97, bf16[256,768]{1,0:T(8,128)(2,1)S(1)} %get-tuple-element.97, ...), branch_computations={%region_15.0_spmd, %region_16.0_spmd, %region_17.0_spmd, %region_1... | conditional | bytes 1572912 | solution.py:39
  121.4 9.6 %collective-permute-done.17 = bf16[256,768]{1,0:T(8,128)(2,1)} collective-permute-done((bf16[256,768]{1,0:T(8,128)(2,1)S(1)}, bf16[256,768]{1,0:T(8,128)(2,1)}, u32[]{:S(2)}, u32[]{:S(2)}) %collective-permute-start.17) | collective-permute-done | bytes 393248 | tf_op jit(solution)/shard_map/cond/branch_2_fun/ppermute | solution.py:37
  131.9 2.8 %outer.1 = (bf16[256,768]{1,0:T(8,128)(2,1)}, f32[256,768]{1,0:T(8,128)}) custom-call(f32[256,768]{1,0:T(8,128)S(1)} %bitcast.10, bf16[256,768]{1,0:T(8,128)(2,1)} %copy-done.17, bf16[256,768]{1,0:T(8,128)(2,1)S(1)} %copy-done.13, bf16[256,768]{1,0:T(8,128)(2,1)} %get-tuple-element.107.slow_partner, bf16[256,768]{1,0:T(8,128)(2,1)} %get-tuple-element.108.grad_partner, ...), custom_call_target="tpu_custom_call" | custom-call | bytes 2097152 | tf_op jit(solution)/shard_map/outer/pallas_call | solution.py:229
  134.7 2.6 %multiply_convert_fusion = bf16[512,768]{1,0:T(8,128)(2,1)} fusion(f32[512,768]{1,0:T(8,128)S(1)} %copy-done.16, f32[512,768]{1,0:T(8,128)S(1)} %up.2, f32[512,768]{1,0:T(8,128)} %collective-permute-done.39), kind=kLoop, calls=%fused_computation.13 | loop fusion | flops 1179648 | bytes 5505024 | tf_op jit(solution)/shard_map/convert_element_type | solution.py:285
  (81 shorter events, 23.8 us)
Async XLA Ops:
  5.1 44.9 %collective-permute-start.38 = (bf16[512,2048]{1,0:T(8,128)(2,1)}, bf16[512,2048]{1,0:T(8,128)(2,1)S(1)}, u32[]{:S(2)}, u32[]{:S(2)}) collective-permute-start(bf16[512,2048]{1,0:T(8,128)(2,1)} %get-tuple-element.86), channel_id=1, source_target_pairs={{0,1},{1,0},{2,3},{3,2},{4,5},{5,4},{6,7},{7,6},{8,9},{9,8},{10,11... | collective-permute-start | bytes 6291464 | tf_op jit(solution)/shard_map/ppermute | solution.py:27
  5.3 55.4 %copy-start.17 = (bf16[256,768]{1,0:T(8,128)(2,1)}, bf16[256,768]{1,0:T(8,128)(2,1)S(1)}, u32[]{:S(2)}) copy-start(bf16[256,768]{1,0:T(8,128)(2,1)S(1)} %get-tuple-element.95.fast) | copy-start | bytes 1179652
  5.3 7.9 %collective-permute-start.34 = (bf16[256,384]{1,0:T(8,128)(2,1)S(1)}, bf16[256,384]{1,0:T(8,128)(2,1)S(1)}, u32[]{:S(2)}, u32[]{:S(2)}) collective-permute-start(bf16[256,384]{1,0:T(8,128)(2,1)S(1)} %get-tuple-element.85.refs_0_), channel_id=1, source_target_pairs={{0,4},{4,0},{8,12},{12,8},{1,5},{5,1},{9,13},{13,9},{2,6},{6,2},{1... | collective-permute-start | bytes 589832 | tf_op jit(solution)/shard_map/ppermute | solution.py:31
  6.9 12.3 %collective-permute-start.35 = (bf16[256,384]{1,0:T(8,128)(2,1)S(1)}, bf16[256,384]{1,0:T(8,128)(2,1)S(1)}, u32[]{:S(2)}, u32[]{:S(2)}) collective-permute-start(bf16[256,384]{1,0:T(8,128)(2,1)S(1)} %get-tuple-element.85.refs_0_), channel_id=1, source_target_pairs={{0,8},{4,12},{8,0},{12,4},{1,9},{5,13},{9,1},{13,5},{2,10},{6,14},... | collective-permute-start | bytes 589832 | tf_op jit(solution)/shard_map/ppermute | solution.py:31
  9.6 12.1 %collective-permute-start.36 = (bf16[256,384]{1,0:T(8,128)(2,1)S(1)}, bf16[256,384]{1,0:T(8,128)(2,1)S(1)}, u32[]{:S(2)}, u32[]{:S(2)}) collective-permute-start(bf16[256,384]{1,0:T(8,128)(2,1)S(1)} %get-tuple-element.85.refs_0_), channel_id=1, source_target_pairs={{0,12},{4,8},{8,4},{12,0},{1,13},{5,9},{9,5},{13,1},{2,14},{6,10},... | collective-permute-start | bytes 589832 | tf_op jit(solution)/shard_map/ppermute | solution.py:31
  10.1 13.4 %collective-permute-start.30 = (bf16[256,384]{1,0:T(8,128)(2,1)S(1)}, bf16[256,384]{1,0:T(8,128)(2,1)S(1)}, u32[]{:S(2)}, u32[]{:S(2)}) collective-permute-start(bf16[256,384]{1,0:T(8,128)(2,1)S(1)} %get-tuple-element.84.refs_0_), channel_id=1, source_target_pairs={{0,2},{2,0},{1,3},{3,1},{4,6},{6,4},{5,7},{7,5},{8,10},{10,8},{9,1... | collective-permute-start | bytes 589832 | tf_op jit(solution)/shard_map/ppermute | solution.py:27
  21.8 28.2 %collective-permute-start.37 = (bf16[1024,384]{1,0:T(8,128)(2,1)S(1)}, bf16[1024,384]{1,0:T(8,128)(2,1)S(1)}, u32[]{:S(2)}, u32[]{:S(2)}) collective-permute-start(bf16[1024,384]{1,0:T(8,128)(2,1)S(1)} %join.3.near), channel_id=1, source_target_pairs={{0,2},{2,0},{1,3},{3,1},{4,6},{6,4},{5,7},{7,5},{8,10},{10,8},{9,1... | collective-permute-start | bytes 2359304 | tf_op jit(solution)/shard_map/ppermute | solution.py:27
  23.5 12.1 %collective-permute-start.31 = (bf16[512,384]{1,0:T(8,128)(2,1)S(1)}, bf16[512,384]{1,0:T(8,128)(2,1)S(1)}, u32[]{:S(2)}, u32[]{:S(2)}) collective-permute-start(bf16[512,384]{1,0:T(8,128)(2,1)S(1)} %join.2.pair), channel_id=1, source_target_pairs={{0,4},{4,0},{8,12},{12,8},{1,5},{5,1},{9,13},{13,9},{2,6},{6,2},{1... | collective-permute-start | bytes 1179656 | tf_op jit(solution)/shard_map/ppermute | solution.py:31
  25.6 28.6 %copy-start.3 = (bf16[512,2048]{1,0:T(8,128)(2,1)S(1)}, bf16[512,2048]{1,0:T(8,128)(2,1)}, u32[]{:S(2)}) copy-start(bf16[512,2048]{1,0:T(8,128)(2,1)} %get-tuple-element.83.tokens.own_tokens) | copy-start | bytes 6291460
  25.6 28.6 %collective-permute-start.40 = (bf16[512,768]{1,0:T(8,128)(2,1)S(1)}, bf16[512,768]{1,0:T(8,128)(2,1)S(1)}, u32[]{:S(2)}, u32[]{:S(2)}) collective-permute-start(bf16[512,768]{1,0:T(8,128)(2,1)S(1)} %get-tuple-element.88.own_grads), channel_id=1, source_target_pairs={{0,1},{1,0},{2,3},{3,2},{4,5},{5,4},{6,7},{7,6},{8,9},{9,8},{10,11... | collective-permute-start | bytes 2359304 | tf_op jit(solution)/shard_map/ppermute | solution.py:27
  25.6 16.3 %collective-permute-start.32 = (bf16[512,384]{1,0:T(8,128)(2,1)S(1)}, bf16[512,384]{1,0:T(8,128)(2,1)S(1)}, u32[]{:S(2)}, u32[]{:S(2)}) collective-permute-start(bf16[512,384]{1,0:T(8,128)(2,1)S(1)} %join.2.pair), channel_id=1, source_target_pairs={{0,8},{4,12},{8,0},{12,4},{1,9},{5,13},{9,1},{13,5},{2,10},{6,14},... | collective-permute-start | bytes 1179656 | tf_op jit(solution)/shard_map/ppermute | solution.py:31
  35.6 18.5 %copy-start.5 = (bf16[512,384]{1,0:T(8,128)(2,1)}, bf16[512,384]{1,0:T(8,128)(2,1)S(1)}, u32[]{:S(2)}) copy-start(bf16[512,384]{1,0:T(8,128)(2,1)S(1)} %collective-permute-done.31.x1) | copy-start | bytes 1179652
  35.6 14.4 %collective-permute-start.33 = (bf16[512,384]{1,0:T(8,128)(2,1)S(1)}, bf16[512,384]{1,0:T(8,128)(2,1)S(1)}, u32[]{:S(2)}, u32[]{:S(2)}) collective-permute-start(bf16[512,384]{1,0:T(8,128)(2,1)S(1)} %join.2.pair), channel_id=1, source_target_pairs={{0,12},{4,8},{8,4},{12,0},{1,13},{5,9},{9,5},{13,1},{2,14},{6,10},... | collective-permute-start | bytes 1179656 | tf_op jit(solution)/shard_map/ppermute | solution.py:31
  54.1 80.6 %collective-permute-start.39 = (f32[512,768]{1,0:T(8,128)}, f32[512,768]{1,0:T(8,128)}, u32[]{:S(2)}, u32[]{:S(2)}) collective-permute-start(f32[512,768]{1,0:T(8,128)} %up.3), channel_id=1, source_target_pairs={{0,1},{1,0},{2,3},{3,2},{4,5},{5,4},{6,7},{7,6},{8,9},{9,8},{10,11... | collective-permute-start | bytes 4718600 | tf_op jit(solution)/shard_map/ppermute | solution.py:27
  60.2 45.1 %collective-permute-start.44 = (bf16[1024,384]{1,0:T(8,128)(2,1)}, bf16[1024,384]{1,0:T(8,128)(2,1)}, u32[]{:S(2)}, u32[]{:S(2)}) collective-permute-start(bf16[1024,384]{1,0:T(8,128)(2,1)} %get-tuple-element.94), channel_id=1, source_target_pairs={{0,2},{2,0},{1,3},{3,1},{4,6},{6,4},{5,7},{7,5},{8,10},{10,8},{9,1... | collective-permute-start | bytes 2359304 | tf_op jit(solution)/shard_map/ppermute | solution.py:27
  60.7 20.0 %collective-permute-start.2 = (bf16[256,768]{1,0:T(8,128)(2,1)S(1)}, bf16[256,768]{1,0:T(8,128)(2,1)}, u32[]{:S(2)}, u32[]{:S(2)}) collective-permute-start(bf16[256,768]{1,0:T(8,128)(2,1)S(1)} %param.2), channel_id=1, source_target_pairs={{0,48},{16,32},{32,16},{48,0},{64,112},{80,96},{96,80},{112,64},{1... | collective-permute-start | bytes 1179656 | tf_op jit(solution)/shard_map/cond/branch_2_fun/ppermute | solution.py:37
  80.7 12.2 %collective-permute-start.41 = (bf16[512,384]{1,0:T(8,128)(2,1)}, bf16[512,384]{1,0:T(8,128)(2,1)S(1)}, u32[]{:S(2)}, u32[]{:S(2)}) collective-permute-start(bf16[512,384]{1,0:T(8,128)(2,1)} %copy-done.15), channel_id=1, source_target_pairs={{0,4},{4,0},{8,12},{12,8},{1,5},{5,1},{9,13},{13,9},{2,6},{6,2},{1... | collective-permute-start | bytes 1179656 | tf_op jit(solution)/shard_map/ppermute | solution.py:31
  80.7 20.3 %collective-permute-start.42 = (bf16[512,384]{1,0:T(8,128)(2,1)}, bf16[512,384]{1,0:T(8,128)(2,1)S(1)}, u32[]{:S(2)}, u32[]{:S(2)}) collective-permute-start(bf16[512,384]{1,0:T(8,128)(2,1)} %copy-done.14), channel_id=1, source_target_pairs={{0,8},{4,12},{8,0},{12,4},{1,9},{5,13},{9,1},{13,5},{2,10},{6,14},... | collective-permute-start | bytes 1179656 | tf_op jit(solution)/shard_map/ppermute | solution.py:31
  83.8 19.6 %collective-permute-start.43 = (bf16[512,384]{1,0:T(8,128)(2,1)S(1)}, bf16[512,384]{1,0:T(8,128)(2,1)S(1)}, u32[]{:S(2)}, u32[]{:S(2)}) collective-permute-start(bf16[512,384]{1,0:T(8,128)(2,1)S(1)} %get-tuple-element.92), channel_id=1, source_target_pairs={{0,12},{4,8},{8,4},{12,0},{1,13},{5,9},{9,5},{13,1},{2,14},{6,10},... | collective-permute-start | bytes 1179656 | tf_op jit(solution)/shard_map/ppermute | solution.py:31
  103.6 11.1 %collective-permute-start.45 = (bf16[256,384]{1,0:T(8,128)(2,1)S(1)}, bf16[256,384]{1,0:T(8,128)(2,1)S(1)}, u32[]{:S(2)}, u32[]{:S(2)}) collective-permute-start(bf16[256,384]{1,0:T(8,128)(2,1)S(1)} %slice.43), channel_id=1, source_target_pairs={{0,2},{2,0},{1,3},{3,1},{4,6},{6,4},{5,7},{7,5},{8,10},{10,8},{9,1... | collective-permute-start | bytes 589832 | tf_op jit(solution)/shard_map/ppermute | solution.py:27
  106.9 7.8 %collective-permute-start.46 = (bf16[256,384]{1,0:T(8,128)(2,1)S(1)}, bf16[256,384]{1,0:T(8,128)(2,1)S(1)}, u32[]{:S(2)}, u32[]{:S(2)}) collective-permute-start(bf16[256,384]{1,0:T(8,128)(2,1)S(1)} %get-tuple-element.106), channel_id=1, source_target_pairs={{0,4},{4,0},{8,12},{12,8},{1,5},{5,1},{9,13},{13,9},{2,6},{6,2},{1... | collective-permute-start | bytes 589832 | tf_op jit(solution)/shard_map/ppermute | solution.py:31
  107.0 9.9 %collective-permute-start.47 = (bf16[256,384]{1,0:T(8,128)(2,1)S(1)}, bf16[256,384]{1,0:T(8,128)(2,1)S(1)}, u32[]{:S(2)}, u32[]{:S(2)}) collective-permute-start(bf16[256,384]{1,0:T(8,128)(2,1)S(1)} %get-tuple-element.105), channel_id=1, source_target_pairs={{0,8},{4,12},{8,0},{12,4},{1,9},{5,13},{9,1},{13,5},{2,10},{6,14},... | collective-permute-start | bytes 589832 | tf_op jit(solution)/shard_map/ppermute | solution.py:31
  110.1 8.9 %collective-permute-start.48 = (bf16[256,384]{1,0:T(8,128)(2,1)S(1)}, bf16[256,384]{1,0:T(8,128)(2,1)S(1)}, u32[]{:S(2)}, u32[]{:S(2)}) collective-permute-start(bf16[256,384]{1,0:T(8,128)(2,1)S(1)} %get-tuple-element.104), channel_id=1, source_target_pairs={{0,12},{4,8},{8,4},{12,0},{1,13},{5,9},{9,5},{13,1},{2,14},{6,10},... | collective-permute-start | bytes 589832 | tf_op jit(solution)/shard_map/ppermute | solution.py:31
  120.0 10.9 %collective-permute-start.17 = (bf16[256,768]{1,0:T(8,128)(2,1)S(1)}, bf16[256,768]{1,0:T(8,128)(2,1)}, u32[]{:S(2)}, u32[]{:S(2)}) collective-permute-start(bf16[256,768]{1,0:T(8,128)(2,1)S(1)} %param.17), channel_id=1, source_target_pairs={{0,48},{16,32},{32,16},{48,0},{64,112},{80,96},{96,80},{112,64},{1... | collective-permute-start | bytes 1179656 | tf_op jit(solution)/shard_map/cond/branch_2_fun/ppermute | solution.py:37
  (19 other events, 124.7 us)
